TPU v7x, 512 devices: a whole 4x4x16 slice. The times are simulated.
512 devices in a mesh: tiles: 128 (over z, y, core), rep: 4 (over x).
Axes of the slice: x: 4, y: 4, z: 16, core: 2. Of those that a mesh axis runs over, the one named last changes fastest.
Arguments:
- tiles: bfloat16 [1024, 64, 4096], P(('tiles', 'rep')), may hold values from -6 to 6
- block_one: int32 [1024], P(('tiles', 'rep')), may hold values from 0 to 127
- block_two: int32 [1024], P(('tiles', 'rep')), may hold values from 0 to 255
- block_three: int32 [1024], P(('tiles', 'rep')), may hold values from 0 to 15
- owner_map: int32 [128], replicated, may hold values from 0 to 127, each once
- u_one: float32 [32, 8192], P(None, 'tiles'), may hold values from -6 to 6
- u_two: bfloat16 [32, 16384], P(None, 'tiles'), may hold values from -6 to 6
- u_three: bfloat16 [32, 1024], replicated, may hold values from -6 to 6
Outputs:
- factor: float32 [32, 8192], P(None, 'tiles')
- tile_factor: bfloat16 [1024, 2048], P(('tiles', 'rep'))
All inputs are finite; a program needn't handle non-finite values.
Results may differ from a plain program's by a relative error of at most 0.0081.
Values may be sent and summed in bfloat16 or wider, within the bound.
A program may use at most 64 MiB of HBM per device.

v0:
```python
import jax
import jax.numpy as jnp
from jax import lax
from jax.sharding import PartitionSpec as P

NS_STEPS = 2


def pick(table, index, width):
    grid = table.reshape(table.shape[0], -1, width)
    return jnp.transpose(jnp.take(grid, index, axis=1), (1, 0, 2))


def gram_total(local):
    return lax.psum(local, "tiles")


def orthonormal(rows, rows_total):
    hi = lax.Precision.HIGHEST
    rank = rows.shape[0]
    g0 = gram_total(jnp.dot(rows, rows.T, precision=hi, preferred_element_type=jnp.float32))
    msq = jnp.trace(g0) / rows_total
    inv = 1.0 / jnp.sqrt(msq + 1e-06)
    x = rows * inv
    g = g0 * (inv * inv) / rows_total
    eye = jnp.eye(rank, dtype=jnp.float32)
    for step in range(NS_STEPS):
        if step > 0:
            g = (
                gram_total(jnp.dot(x, x.T, precision=hi, preferred_element_type=jnp.float32))
                / rows_total
            )
        x = jnp.dot(1.5 * eye - 0.5 * g, x, precision=hi, preferred_element_type=jnp.float32)
    return x


def spread(current):
    cast = current.astype(jnp.bfloat16)
    return lax.all_gather(cast, "tiles", axis=1, tiled=True)


def per_device(tiles, block_one, block_two, block_three, owner_map, u_one, u_two, u_three):
    hi = lax.Precision.HIGHEST
    count = tiles.shape[0]
    width = tiles.shape[1]
    rank = u_three.shape[0]
    blocks_total = owner_map.shape[0]
    rows_total = blocks_total * width
    two_full = lax.all_gather(u_two, "tiles", axis=1, tiled=True)
    two_pick = pick(two_full, block_two, width)
    three_pick = pick(u_three, block_three, width)
    cube = tiles.reshape(count, width, width, width)
    first = jnp.einsum(
        "tijk,tsk->tijs", cube, three_pick, preferred_element_type=jnp.float32
    ).astype(jnp.bfloat16)
    second = jnp.einsum("tijs,trj->tirs", first, two_pick, preferred_element_type=jnp.float32)
    products = second.reshape(count, width, rank * rank).astype(jnp.bfloat16)
    positions = jnp.take(owner_map, block_one)
    onehot = (positions[:, None] == jnp.arange(blocks_total, dtype=jnp.int32)[None, :]).astype(
        jnp.float32
    )
    current = u_one
    readers = pick(spread(current), positions, width)
    partial_value = jnp.einsum("tic,tri->rc", products, readers, preferred_element_type=jnp.float32)
    project = lax.psum(partial_value, ("tiles", "rep")).astype(jnp.bfloat16)
    z_tile = jnp.einsum("rc,tic->tri", project, products, preferred_element_type=jnp.float32)
    term = jnp.einsum("tri,tn->rni", z_tile, onehot, precision=hi).reshape(rank, rows_total)
    rows = lax.psum_scatter(term, "tiles", scatter_dimension=1, tiled=True)
    rows = lax.psum(rows, "rep")
    current = orthonormal(rows, rows_total)
    tile_factor = pick(spread(current), positions, width).reshape(count, rank * width)
    return (current, tile_factor)


def solution(mesh):
    in_specs = (
        P(("tiles", "rep"), None, None),
        P(("tiles", "rep")),
        P(("tiles", "rep")),
        P(("tiles", "rep")),
        P(),
        P(None, "tiles"),
        P(None, "tiles"),
        P(),
    )
    out_specs = (P(None, "tiles"), P(("tiles", "rep"), None))
    return jax.shard_map(
        per_device, mesh=mesh, in_specs=in_specs, out_specs=out_specs, check_vma=False
    )
```

profile of v0, /device:TPU:1, one launch (start us, length us, event | category | flops | bytes accessed | tf_op | source)
XLA Modules:
  0.0 1633.5 jit_solution(5011610970250502089)
XLA Ops:
  7.2 0.7 all-gather.4.cloned.1.call-update
  8.0 0.7 compare_select_fusion.3
  8.6 0.7 convert_bitcast_fusion.1
  9.3 1.0 reshape.51
  10.4 109.1 %all-gather = bf16[128,64,32]{1,2,0:T(8,128)(2,1)S(1)} all-gather(bf16[1,64,32]{1,2,0:T(8,128)(2,1)S(1)} %convert_bitcast_fusion.1), channel_id=1, replica_groups=mesh['tiles'=128,'rep'=4] {'tiles'}, dimensions={0}, use_global_device_ids=true | all-gather | bytes 528384 | tf_op jit(solution)/shard_map/all_gather | solution.py:39
  119.9 0.8 reshape.103
  120.7 1.1 reshape.53
  121.9 0.7 copy.32
  122.6 3.4 reshape.52
  126.1 0.6 gather_fusion
  126.7 0.6 gather_fusion.2
  128.0 2.0 fusion
  130.0 17.5 %all-gather.4.cloned.1.call-done = bf16[32,16384]{1,0:T(8,128)(2,1)} async-done(((bf16[32,128]{1,0:T(8,128)(2,1)}), bf16[32,16384]{1,0:T(8,128)(2,1)}) %all-gather.4.cloned.1.call-update) | async-done | bytes 1048592 | tf_op jit(solution)/shard_map/all_gather | solution.py:49
  147.5 3.0 reshape.50
  150.6 2.7 copy.27
  153.3 2.1 gather_fusion.1
  155.4 1.1 fusion.1
  157.0 102.8 %all-reduce.1 = bf16[32,1024]{1,0:T(8,128)(2,1)S(1)} all-reduce(f32[32,1024]{1,0:T(8,128)S(1)} %convolution_bitcast_fusion.1), channel_id=1, replica_groups=mesh['tiles'=128,'rep'=4] {'tiles','rep'}, use_global_device_ids=true, to_apply=%region_0.0 | all-reduce | flops 32768 | bytes 196608 | tf_op jit(solution)/shard_map/psum | solution.py:65
  259.9 1.0 convolution_bitcast_fusion
  261.0 4.4 copy.45
  265.5 245.9 %reduce-scatter.4.cloned.1.call-done = f32[64,32]{1,0:T(8,128)} async-done(((f32[8192,32]{1,0:T(8,128)}), f32[64,32]{1,0:T(8,128)}) %reduce-scatter.4.cloned.1.call-update) | async-done | bytes 8208
  511.3 0.8 copy.44
  512.2 13.3 psum.29
  525.6 500.6 %psum.30 = f32[32,32]{1,0:T(8,128)S(1)} all-reduce(f32[32,32]{1,0:T(8,128)S(1)} %fusion.44), channel_id=1, replica_groups=mesh['tiles'=128,'rep'=4] {'tiles'}, use_global_device_ids=true, to_apply=%region_3.5 | all-reduce | flops 1024 | bytes 8192 | tf_op jit(solution)/shard_map/psum | solution.py:15
  1026.3 0.6 select_reduce_fusion
  1027.9 490.9 %psum.31 = f32[32,32]{1,0:T(8,128)S(1)} all-reduce(f32[32,32]{1,0:T(8,128)S(1)} %fusion.45), channel_id=1, replica_groups=mesh['tiles'=128,'rep'=4] {'tiles'}, use_global_device_ids=true, to_apply=%region_5.7 | all-reduce | flops 1024 | bytes 8192 | tf_op jit(solution)/shard_map/psum | solution.py:15
  1518.9 103.3 %all-gather.1 = bf16[128,64,32]{1,2,0:T(8,128)(2,1)S(1)} all-gather(bf16[1,64,32]{1,2,0:T(8,128)(2,1)S(1)} %convert_bitcast_fusion), channel_id=1, replica_groups=mesh['tiles'=128,'rep'=4] {'tiles'}, dimensions={0}, use_global_device_ids=true | all-gather | bytes 528384 | tf_op jit(solution)/shard_map/all_gather | solution.py:39
  1622.6 0.8 reshape.105
  1623.5 1.1 reshape.55
  1624.6 0.7 copy.38
  1625.3 0.6 gather_fusion.4
  1625.9 0.7 reshape.56
  (36 shorter events, 2.9 us)
Async XLA Ops:
  7.2 118.9 %copy-start = (s32[128]{0:T(128)S(1)}, s32[128]{0:T(128)}, u32[]{:S(2)}) copy-start(s32[128]{0:T(128)} %param.14) | copy-start | bytes 1540
  7.2 140.3 %all-gather.4.cloned.1.call-start = ((), (), s32[]{:S(2)}) async-start(), calls=%async_computation.1 | async-start | bytes 1056768 | tf_op jit(solution)/shard_map/all_gather | solution.py:49
  7.9 503.4 %reduce-scatter.4.cloned.1.call-start = ((), (), s32[]{:S(2)}) async-start(), calls=%async_computation.2 | async-start | bytes 4227072
  122.6 4.2 copy-start.4
  122.6 4.7 copy-start.2
  122.6 5.3 copy-start.3
  1518.9 104.6 %copy-start.1 = (f32[32,64]{1,0:T(8,128)}, f32[32,64]{1,0:T(8,128)S(1)}, u32[]{:S(2)}) copy-start(f32[32,64]{1,0:T(8,128)S(1)} %fusion.7) | copy-start | bytes 24580
Sparse Core Ops, SparseCore 0:
  11.0 136.4 all-gather.3
  265.6 245.7 reduce-scatter.3
where the time goes:
time: 1630 us
  blocking collectives  1320 us (81%)
  waiting for transfers between devices  264 us (16%)
  local copies, waits for them, and re-layouts  27 us (2%)
    psum x2, blocking collectives, gram_total(): return lax.psum(local, 'tiles')  992 us
    unnamed x3, waiting for transfers between devices  247 us
    all_gather x2, blocking collectives, spread(): return lax.all_gather(cast, 'tiles', axis=1, tiled=True)  212 us
    psum x1, blocking collectives, per_device(): project = lax.psum(partial_value, ('tiles', 'rep')).astype(jnp.bfloat16)  103 us
  transfers between devices with their start and end apart: 2, of which 2 were waited for; matrix products, arithmetic and copies ran while one was open for 1% of the time, Pallas kernels for 0%

commit v1 on v0

v1 whole, which is shorter than its diff:
```python
import functools

import jax
import jax.numpy as jnp
from jax import lax
from jax.experimental import pallas as pl
from jax.experimental.pallas import tpu as pltpu
from jax.sharding import PartitionSpec as P

MESH = pl.DeviceIdType.MESH
NS_STEPS = 2
YC = 8
F32 = jnp.float32
BF16 = jnp.bfloat16
HI = lax.Precision.HIGHEST


def iota(shape, dim):
    return lax.broadcasted_iota(jnp.int32, shape, dim)


def nt(a, b, precision=None):
    return lax.dot_general(
        a, b, (((1,), (1,)), ((), ())), precision=precision, preferred_element_type=F32
    )


def kernel(
    nx, nz, rows_total,
    tiles_ref, b1_ref, b2_ref, b3_ref, owner_ref, u1_ref, u2_ref, u3_ref,
    factor_ref, tf_ref,
    tl, us, shq, tq, req, reqs, obuf, gbuf, ft, pt, wsend, wrecv, lsend, lrecv, psend, precv,
    zsend, zrecv, ysend, yrecv, gsend, grecv, ssend, srecv, xsend, xrecv, mref,
    tsem, send, recv,
):
    pln = nx * YC
    per = nz // nx
    qr = 32 // nx
    t_id = lax.axis_index("tiles")
    x = lax.axis_index("rep")
    z = lax.div(t_id, YC)
    yc = lax.rem(t_id, YC)
    m = x * YC + yc

    copies = [
        pltpu.make_async_copy(tiles_ref.at[t], tl.at[pl.ds(64 * t, 64)], tsem.at[t])
        for t in range(2)
    ]
    for c in copies:
        c.start()

    def mate(k):
        w = lax.rem(m + k, pln)
        return w, {"tiles": z * YC + lax.rem(w, YC), "rep": lax.div(w, YC)}

    def peer(k):
        w = lax.rem(z + k, nz)
        return w, {"tiles": w * YC + yc, "rep": x}

    def xmate(k):
        w = lax.rem(x + k, nx)
        return w, {"tiles": t_id, "rep": w}

    barrier = pltpu.get_barrier_semaphore()

    def greet(who, n):
        def body(k, carry):
            pl.semaphore_signal(barrier, inc=1, device_id=who(k)[1], device_id_type=MESH)
            return carry

        lax.fori_loop(1, n, body, 0)

    greet(mate, pln)
    greet(peer, nz)

    def post(who, n, phase, src, dst):
        def body(k, carry):
            w, device = who(k)
            pltpu.make_async_remote_copy(
                src_ref=src(w), dst_ref=dst, send_sem=send.at[phase], recv_sem=recv.at[phase],
                device_id=device, device_id_type=MESH,
            ).start()
            return carry

        lax.fori_loop(1, n, body, 0)

    def land(buf, n, phase):
        part = buf.at[pl.ds(0, n - 1)]
        pltpu.make_async_copy(part, part, recv.at[phase]).wait()

    def sent(buf, n, phase):
        part = buf.at[pl.ds(0, n - 1)]
        pltpu.make_async_copy(part, part, send.at[phase]).wait()

    b2 = [b2_ref[t] for t in range(2)]
    b3 = [b3_ref[t] for t in range(2)]
    pos = [owner_ref[b1_ref[t]] for t in range(2)]

    r16 = iota((16, 128), 0)
    l16 = iota((16, 128), 1)

    def ask(q0, q1):
        want = jnp.where(r16 < qr, q0 * qr, q1 * qr - qr) + r16
        return jnp.where(l16 == want, 1.0, 0.0).astype(BF16)

    reqs[pl.ds(0, 16), :] = ask(lax.shift_right_logical(b2[0], 4), lax.shift_right_logical(b2[1], 4))
    reqs[pl.ds(16, 16), :] = ask(lax.shift_right_logical(pos[0], 3), lax.shift_right_logical(pos[1], 3))
    reqs[pl.ds(32, 16), :] = jnp.where(l16 < 64, pos[0], pos[1]).astype(F32).astype(BF16)
    us[:, pl.ds(0, 128)] = u2_ref[...].astype(F32)
    us[:, pl.ds(128, 64)] = u1_ref[...]
    us[:, pl.ds(192, 64)] = jnp.zeros((32, 64), F32)
    shq[...] = us[pl.ds(pl.multiple_of(x * qr, qr), qr), :].astype(BF16)

    pl.semaphore_wait(barrier, pln + nz - 2)
    post(peer, nz, 0, lambda w: shq, tq.at[z])
    post(mate, pln, 1, lambda w: reqs, req.at[m])
    tq[z] = shq[...]
    req[m] = reqs[...]

    lane128 = iota((32, 128), 1)
    spread = jnp.where(iota((256, 32), 0) // 8 == iota((256, 32), 1), 1.0, 0.0).astype(BF16)
    diag = []
    for t in range(2):
        chunk = jnp.zeros((32, 128), F32)
        for q in range(8):
            part = u3_ref[:, q * 128 : (q + 1) * 128].astype(F32)
            chunk = chunk + jnp.where(lax.shift_right_logical(b3[t], 1) == q, part, 0.0)
        swapped = pltpu.roll(chunk, 64, 1)
        odd = lax.rem(b3[t], 2) == 1
        twice = jnp.where((lane128 < 64) != odd, chunk, swapped)
        wide = jnp.dot(spread, twice.astype(BF16), preferred_element_type=F32)
        row = lax.rem(iota((256, 128), 0), 8)
        half = jnp.where(iota((256, 128), 1) < 64, 0, 1)
        diag.append(
            jnp.concatenate(
                [jnp.where(row == half + 2 * q, wide, 0.0).astype(BF16) for q in range(4)], axis=1
            )
        )
    for c in copies:
        c.wait()
    low256 = iota((256, 128), 1) < 64
    for jc in range(8):
        block = tl[:, jc * 512 : (jc + 1) * 512]
        out = jnp.where(low256, nt(diag[0], block), nt(diag[1], block))
        ft[:, jc * 8 : (jc + 1) * 8, :] = out.reshape(32, 8, 128)

    land(tq, nz, 0)
    land(req, pln, 1)
    table = tq[...].astype(F32).reshape(nz * qr, 256).astype(BF16)
    two_part = jnp.dot(
        req[:, 0:16, :].reshape(pln * 16, 128), table[:, 0:128], preferred_element_type=F32
    )
    one_part = jnp.dot(
        req[:, 16:32, :].reshape(pln * 16, 128), table[:, 128:256], preferred_element_type=F32
    )
    obuf[:, 0:16, :] = two_part.reshape(pln, 16, 128).astype(BF16)
    obuf[:, 16:32, :] = one_part.reshape(pln, 16, 128).astype(BF16)
    post(mate, pln, 2, lambda w: obuf.at[w], gbuf.at[m])
    gbuf[m] = obuf[m]
    land(gbuf, pln, 2)

    r32 = iota((32, 128), 0)
    holder = jnp.where(
        r32 < 16,
        jnp.where(r32 < 8, lax.rem(lax.shift_right_logical(b2[0], 1), YC),
                  lax.rem(lax.shift_right_logical(b2[1], 1), YC)),
        jnp.where(r32 < 24, lax.rem(pos[0], YC), lax.rem(pos[1], YC)),
    )
    parts = []
    for xx in range(nx):
        acc = jnp.zeros((32, 128), F32)
        for cc in range(YC):
            acc = acc + jnp.where(holder == cc, gbuf[xx * YC + cc].astype(F32), 0.0)
        parts.append(acc)

    def rows_of(slot):
        return jnp.concatenate([p[slot * 8 : slot * 8 + 8] for p in parts], axis=0)

    low = lane128 < 64
    two = []
    for t in range(2):
        v = rows_of(t)
        two.append(jnp.where(lax.rem(b2[t], 2) == 1, pltpu.roll(v, 64, 1), v))
    u2 = jnp.concatenate(two, axis=0)[:, 0:64].astype(BF16)
    readers = jnp.where(low, rows_of(2), pltpu.roll(rows_of(3), 64, 1)).astype(BF16)

    for s in range(32):
        d = jnp.dot(u2, ft[s].astype(BF16), preferred_element_type=F32)
        pt[s * 32 : (s + 1) * 32, :] = jnp.where(low, d[0:32], d[32:64]).astype(BF16)

    w_part = nt(readers, pt[...])
    for q in range(8):
        wsend[:, q, :] = w_part[:, q * 128 : (q + 1) * 128]
    post(mate, pln, 3, lambda w: wsend.at[w], wrecv.at[m])
    wrecv[m] = wsend[m]
    land(wrecv, pln, 3)
    lsend[...] = jnp.sum(wrecv[...], axis=0)
    post(peer, nz, 4, lambda w: lsend, lrecv.at[z])
    lrecv[z] = lsend[...]
    land(lrecv, nz, 4)
    psend[...] = jnp.sum(lrecv[...], axis=0).astype(BF16).astype(F32)
    post(mate, pln, 5, lambda w: psend, precv.at[m])
    precv[m] = psend[...]
    land(precv, pln, 5)
    project = jnp.concatenate([precv[:, q, :].astype(BF16) for q in range(8)], axis=1)

    zsend[...] = jnp.dot(project, pt[...], preferred_element_type=F32).astype(BF16)
    post(mate, pln, 6, lambda w: zsend, zrecv.at[m])
    zrecv[m] = zsend[...]
    land(zrecv, pln, 6)
    sums = [jnp.zeros((32, 128), F32) for _ in range(per)]
    where_to = []
    for w in range(pln):
        goes = req[w, 32:48, :].astype(F32)[0:8]
        goes = jnp.concatenate([goes] * 4, axis=0)
        where_to.append(goes)
        val = zrecv[w].astype(F32)
        for k in range(per):
            mine = ((x * per + k) * YC + yc).astype(F32)
            sums[k] = sums[k] + jnp.where(goes == mine, val, 0.0)
    sums = [v + pltpu.roll(v, 64, 1) for v in sums]
    for k in range(0, per, 2):
        ysend[:, k * 64 : k * 64 + 128] = jnp.where(low, sums[k], sums[k + 1]).astype(BF16)
    post(peer, nz, 7, lambda w: ysend, yrecv.at[z])
    yrecv[z] = ysend[...]
    land(yrecv, nz, 7)
    total = yrecv[0].astype(F32)
    for w in range(1, nz):
        total = total + yrecv[w].astype(F32)

    gw = nt(total, jnp.concatenate([total] * 4, axis=0), HI)
    lane8 = lax.shift_right_logical(iota((8, 128), 1), 5)
    packed = jnp.zeros((8, 128), F32)
    for q in range(4):
        packed = packed + jnp.where(lane8 == q, gw[q * 8 : q * 8 + 8], 0.0)
    gsend[...] = packed
    post(mate, pln, 8, lambda w: gsend, grecv.at[m])
    grecv[m] = packed
    blocks = []
    for k in range(per):
        pair = total[:, (k // 2) * 128 : (k // 2) * 128 + 128]
        other = pltpu.roll(pair, 64, 1)
        blocks.append(jnp.where(low, pair, other) if k % 2 == 0 else jnp.where(low, other, pair))
    for w in range(pln):
        val = jnp.zeros((32, 128), F32)
        for k in range(per):
            mine = ((x * per + k) * YC + yc).astype(F32)
            val = val + jnp.where(where_to[w] == mine, blocks[k], 0.0)
        ssend[w] = val.astype(BF16)
    post(mate, pln, 9, lambda w: ssend.at[w], srecv.at[m])
    srecv[m] = ssend[m]
    own = jnp.zeros((32, 128), F32)
    for k in range(per):
        own = own + jnp.where(lax.rem(z, per) == k, blocks[k], 0.0)
    xsend[...] = own
    post(xmate, nx, 10, lambda w: xsend, xrecv.at[x])
    xrecv[x] = own

    land(grecv, pln, 8)
    packed = jnp.sum(grecv[...], axis=0)
    tall = jnp.concatenate([jnp.where(lane8 == q, packed, 0.0) for q in range(4)], axis=0)
    fold = jnp.where(
        jnp.bitwise_and(iota((128, 32), 0), 31) == iota((128, 32), 1), 1.0, 0.0
    )
    g0 = jnp.dot(tall, fold, precision=HI, preferred_element_type=F32)
    eye = jnp.where(iota((32, 32), 0) == iota((32, 32), 1), 1.0, 0.0)
    trace = jnp.sum(jnp.sum(g0 * eye, axis=1, keepdims=True), axis=0, keepdims=True)
    inv = 1.0 / jnp.sqrt(trace / rows_total + 1e-06)
    g = g0 * (inv * inv) / rows_total
    move = eye * inv
    for step in range(NS_STEPS):
        if step > 0:
            g = jnp.dot(
                jnp.dot(a, g, precision=HI, preferred_element_type=F32), a,
                precision=HI, preferred_element_type=F32,
            )
        a = 1.5 * eye - 0.5 * g
        move = jnp.dot(a, move, precision=HI, preferred_element_type=F32)
    mref[:, 0:32] = move

    land(srecv, pln, 9)
    land(xrecv, nx, 10)
    got = srecv[0].astype(F32)
    for w in range(1, pln):
        got = got + srecv[w].astype(F32)
    mine = xrecv[lax.div(z, per)]
    factor_ref[...] = jnp.dot(move, mine[:, 0:64], precision=HI, preferred_element_type=F32)
    order = jnp.concatenate(
        [mref[pl.ds(0, 16, stride=2), :][:, 0:32], mref[pl.ds(1, 16, stride=2), :][:, 0:32]], axis=0
    )
    other = pltpu.roll(got, 64, 1)
    low16 = iota((16, 128), 1) < 64
    for t in range(2):
        both = jnp.where(low, got, other) if t == 0 else jnp.where(low, other, got)
        v = jnp.dot(order, both, precision=HI, preferred_element_type=F32)
        tf_ref[t] = jnp.where(low16, v[0:16], v[16:32]).astype(BF16)

    sent(tq, nz, 0)
    sent(req, pln, 1)
    sent(gbuf, pln, 2)
    sent(wrecv, pln, 3)
    sent(lrecv, nz, 4)
    sent(precv, pln, 5)
    sent(zrecv, pln, 6)
    sent(yrecv, nz, 7)
    sent(grecv, pln, 8)
    sent(srecv, pln, 9)
    sent(xrecv, nx, 10)


def solution(mesh):
    nx = mesh.shape["rep"]
    nz = mesh.shape["tiles"] // YC
    pln = nx * YC
    qr = 32 // nx
    per = nz // nx

    def per_device(tiles, block_one, block_two, block_three, owner_map, u_one, u_two, u_three):
        rows_total = owner_map.shape[0] * tiles.shape[1]
        vm = pl.BlockSpec(memory_space=pltpu.VMEM)
        sm = pl.BlockSpec(memory_space=pltpu.SMEM)
        factor, tf = pl.pallas_call(
            functools.partial(kernel, nx, nz, rows_total),
            out_shape=(
                jax.ShapeDtypeStruct((32, 64), F32),
                jax.ShapeDtypeStruct((2, 16, 128), BF16),
            ),
            in_specs=[pl.BlockSpec(memory_space=pl.ANY), sm, sm, sm, sm, vm, vm, vm],
            out_specs=(vm, vm),
            scratch_shapes=[
                pltpu.VMEM((128, 4096), BF16),
                pltpu.VMEM((32, 256), F32),
                pltpu.VMEM((qr, 256), BF16),
                pltpu.VMEM((nz, qr, 256), BF16),
                pltpu.VMEM((pln, 48, 128), BF16),
                pltpu.VMEM((48, 128), BF16),
                pltpu.VMEM((pln, 32, 128), BF16),
                pltpu.VMEM((pln, 32, 128), BF16),
                pltpu.VMEM((32, 64, 128), F32),
                pltpu.VMEM((1024, 128), BF16),
                pltpu.VMEM((pln, 8, 128), F32),
                pltpu.VMEM((pln, 8, 128), F32),
                pltpu.VMEM((8, 128), F32),
                pltpu.VMEM((nz, 8, 128), F32),
                pltpu.VMEM((8, 128), F32),
                pltpu.VMEM((pln, 8, 128), F32),
                pltpu.VMEM((32, 128), BF16),
                pltpu.VMEM((pln, 32, 128), BF16),
                pltpu.VMEM((32, 64 * per), BF16),
                pltpu.VMEM((nz, 32, 64 * per), BF16),
                pltpu.VMEM((8, 128), F32),
                pltpu.VMEM((pln, 8, 128), F32),
                pltpu.VMEM((pln, 32, 128), BF16),
                pltpu.VMEM((pln, 32, 128), BF16),
                pltpu.VMEM((32, 128), F32),
                pltpu.VMEM((nx, 32, 128), F32),
                pltpu.VMEM((32, 128), F32),
                pltpu.SemaphoreType.DMA((2,)),
                pltpu.SemaphoreType.DMA((11,)),
                pltpu.SemaphoreType.DMA((11,)),
            ],
            compiler_params=pltpu.CompilerParams(
                collective_id=0, has_side_effects=True, vmem_limit_bytes=32 << 20
            ),
            name="hooi_step",
        )(tiles, block_one, block_two, block_three, owner_map, u_one, u_two, u_three)
        return factor, tf.reshape(2, 2048)

    in_specs = (
        P(("tiles", "rep"), None, None),
        P(("tiles", "rep")),
        P(("tiles", "rep")),
        P(("tiles", "rep")),
        P(),
        P(None, "tiles"),
        P(None, "tiles"),
        P(),
    )
    out_specs = (P(None, "tiles"), P(("tiles", "rep"), None))
    return jax.shard_map(
        per_device, mesh=mesh, in_specs=in_specs, out_specs=out_specs, check_vma=False
    )
```

time: 1630 us -> 93.5 us (0.06)
  blocking collectives: 1320 us -> 0 us
  waiting for transfers between devices: 264 us -> 0 us
  Pallas kernels: 0 us -> 85.2 us
  local copies, waits for them, and re-layouts: 27 us -> 7.3 us
    psum x4 -> x0, blocking collectives: 1110 us -> none  [the longest x2 992 us: gram_total(): return lax.psum(local, 'tiles')]
    unnamed x3 -> x0, waiting for transfers between devices: 247 us -> none
    all_gather x2 -> x0, blocking collectives: 212 us -> none  [spread(): return lax.all_gather(cast, 'tiles', axis=1, tiled=True)]
    pallas_call x0 -> x1, Pallas kernels: none -> 85.2 us  [per_device(): pl.pallas_call(functools.partial(kernel, nx, nz, rows_total), out_shape=(...]
    all_gather x1 -> x0, waiting for transfers between devices: 17.5 us -> none  [per_device(): two_full = lax.all_gather(u_two, 'tiles', axis=1, tiled=True)]
  transfers between devices with their start and end apart: 2 -> 0, of which waited for: 2 -> 0; matrix products, arithmetic and copies ran while one was open for 1% -> 0% of each run, Pallas kernels for 0% -> 0%
where the time goes in v1:
time: 93.5 us; the launch traced here: 93.2 us
  Pallas kernels  85.2 us (91%)
  local copies, waits for them, and re-layouts  7.3 us (8%)
    pallas_call x1, Pallas kernels, per_device(): pl.pallas_call(functools.partial(kernel, nx, nz, rows_total), out_shape=(...  85.2 us
    unnamed x18, local copies, waits for them, and re-layouts  7.3 us

profile of v1, /device:TPU:1, one launch (start us, length us, event | category | flops | bytes accessed | tf_op | source)
XLA Modules:
  0.0 93.2 jit_solution(10187416006846069047)
XLA Ops:
  0.6 0.0 copy-start
  0.6 1.2 %copy-done = bf16[2,64,4096]{2,1,0:T(8,128)(2,1)S(1)} copy-done((bf16[2,64,4096]{2,1,0:T(8,128)(2,1)S(1)}, bf16[2,64,4096]{2,1,0:T(8,128)(2,1)}, u32[]{:S(2)}) %copy-start) | copy-done | bytes 1048600
  1.9 0.0 copy-start.1
  1.9 0.8 copy-done.1
  2.7 0.0 copy-start.2
  2.7 0.7 copy-done.2
  3.4 0.0 copy-start.3
  3.4 0.7 copy-done.3
  4.1 0.0 copy-start.4
  4.1 0.7 copy-done.4
  4.8 0.0 copy-start.5
  4.8 0.7 copy-done.5
  5.4 0.0 copy-start.6
  5.4 0.7 copy-done.6
  6.1 0.0 copy-start.7
  6.1 0.7 copy-done.7
  6.7 85.2 %hooi_step.1 = (f32[32,64]{1,0:T(8,128)S(1)}, bf16[2,16,128]{2,1,0:T(8,128)(2,1)S(1)}) custom-call(bf16[2,64,4096]{2,1,0:T(8,128)(2,1)S(1)} %copy-done, s32[2]{0:T(128)S(1)} %copy-done.4, s32[2]{0:T(128)S(1)} %copy-done.5, s32[2]{0:T(128)S(1)} %copy-done.6, s32[128]{0:T(128)S(1)} %copy-done.7, f32[32,64]{1,0:T(8,128)S(1)} %copy-done.2, ...), custom_call_target="tpu_custom_call" | custom-call | tf_op jit(solution)/shard_map/hooi_step/pallas_call | solution.py:322
  92.0 0.6 copy.12
  92.6 0.6 copy.14
Async XLA Ops:
  0.6 1.2 %copy-start = (bf16[2,64,4096]{2,1,0:T(8,128)(2,1)S(1)}, bf16[2,64,4096]{2,1,0:T(8,128)(2,1)}, u32[]{:S(2)}) copy-start(bf16[2,64,4096]{2,1,0:T(8,128)(2,1)} %tiles_ref.1) | copy-start | bytes 3145732
  1.9 0.8 copy-start.1
  2.7 0.7 copy-start.2
  3.4 0.7 copy-start.3
  4.1 0.7 copy-start.4
  4.8 0.7 copy-start.5
  5.4 0.7 copy-start.6
  6.1 0.7 copy-start.7

commit v2 on v1

--- a/solution.py
+++ b/solution.py
@@ -27,10 +27,11 @@
 
 def kernel(
     nx, nz, rows_total,
-    tiles_ref, b1_ref, b2_ref, b3_ref, owner_ref, u1_ref, u2_ref, u3_ref,
+    tiles_ref, b1_hbm, b2_hbm, b3_hbm, owner_hbm, u1_hbm, u2_hbm, u3_hbm,
     factor_ref, tf_ref,
+    b1_ref, b2_ref, b3_ref, owner_ref, u1_ref, u2_ref, u3_ref,
     tl, us, shq, tq, req, reqs, obuf, gbuf, ft, pt, wsend, wrecv, lsend, lrecv, psend, precv,
-    zsend, zrecv, ysend, yrecv, gsend, grecv, ssend, srecv, xsend, xrecv, mref,
+    zsend, zrecv, goes, ysend, yrecv, yall, gsend, grecv, ssend, srecv, xsend, xrecv, mref,
     tsem, send, recv,
 ):
     pln = nx * YC
@@ -46,7 +47,14 @@
         pltpu.make_async_copy(tiles_ref.at[t], tl.at[pl.ds(64 * t, 64)], tsem.at[t])
         for t in range(2)
     ]
-    for c in copies:
+    inputs = [
+        pltpu.make_async_copy(src, dst, tsem.at[2 + n])
+        for n, (src, dst) in enumerate(
+            ((b1_hbm, b1_ref), (owner_hbm, owner_ref), (b2_hbm, b2_ref), (u2_hbm, u2_ref),
+             (u1_hbm, u1_ref), (b3_hbm, b3_ref), (u3_hbm, u3_ref))
+        )
+    ]
+    for c in inputs + copies:
         c.start()
 
     def mate(k):
@@ -92,6 +100,8 @@
         part = buf.at[pl.ds(0, n - 1)]
         pltpu.make_async_copy(part, part, send.at[phase]).wait()
 
+    for c in inputs:
+        c.wait()
     b2 = [b2_ref[t] for t in range(2)]
     b3 = [b3_ref[t] for t in range(2)]
     pos = [owner_ref[b1_ref[t]] for t in range(2)]
@@ -105,7 +115,6 @@
 
     reqs[pl.ds(0, 16), :] = ask(lax.shift_right_logical(b2[0], 4), lax.shift_right_logical(b2[1], 4))
     reqs[pl.ds(16, 16), :] = ask(lax.shift_right_logical(pos[0], 3), lax.shift_right_logical(pos[1], 3))
-    reqs[pl.ds(32, 16), :] = jnp.where(l16 < 64, pos[0], pos[1]).astype(F32).astype(BF16)
     us[:, pl.ds(0, 128)] = u2_ref[...].astype(F32)
     us[:, pl.ds(128, 64)] = u1_ref[...]
     us[:, pl.ds(192, 64)] = jnp.zeros((32, 64), F32)
@@ -154,7 +163,9 @@
         req[:, 16:32, :].reshape(pln * 16, 128), table[:, 128:256], preferred_element_type=F32
     )
     obuf[:, 0:16, :] = two_part.reshape(pln, 16, 128).astype(BF16)
-    obuf[:, 16:32, :] = one_part.reshape(pln, 16, 128).astype(BF16)
+    at = jnp.where(r16 < 8, pos[0], pos[1]).astype(F32)
+    one_part = jnp.where(l16 < 64, one_part.reshape(pln, 16, 128), at)
+    obuf[:, 16:32, :] = one_part.astype(BF16)
     post(mate, pln, 2, lambda w: obuf.at[w], gbuf.at[m])
     gbuf[m] = obuf[m]
     land(gbuf, pln, 2)
@@ -166,11 +177,14 @@
                   lax.rem(lax.shift_right_logical(b2[1], 1), YC)),
         jnp.where(r32 < 24, lax.rem(pos[0], YC), lax.rem(pos[1], YC)),
     )
+    low8 = iota((8, 128), 1) < 64
     parts = []
     for xx in range(nx):
         acc = jnp.zeros((32, 128), F32)
         for cc in range(YC):
-            acc = acc + jnp.where(holder == cc, gbuf[xx * YC + cc].astype(F32), 0.0)
+            val = gbuf[xx * YC + cc].astype(F32)
+            goes[xx * YC + cc] = jnp.where(low8, pltpu.roll(val[16:24], 64, 1), val[24:32])
+            acc = acc + jnp.where(holder == cc, val, 0.0)
         parts.append(acc)
 
     def rows_of(slot):
@@ -208,25 +222,30 @@
     post(mate, pln, 6, lambda w: zsend, zrecv.at[m])
     zrecv[m] = zsend[...]
     land(zrecv, pln, 6)
-    sums = [jnp.zeros((32, 128), F32) for _ in range(per)]
-    where_to = []
+    mine = [((x * per + k) * YC + yc).astype(F32) for k in range(per)]
+    sums = [jnp.zeros((4, 8, 128), F32) for _ in range(per)]
     for w in range(pln):
-        goes = req[w, 32:48, :].astype(F32)[0:8]
-        goes = jnp.concatenate([goes] * 4, axis=0)
-        where_to.append(goes)
-        val = zrecv[w].astype(F32)
-        for k in range(per):
-            mine = ((x * per + k) * YC + yc).astype(F32)
-            sums[k] = sums[k] + jnp.where(goes == mine, val, 0.0)
+        to = goes[w]
+        val = zrecv[w].astype(F32).reshape(4, 8, 128)
+        sums = [v + jnp.where((to == p)[None], val, 0.0) for v, p in zip(sums, mine)]
+    sums = [v.reshape(32, 128) for v in sums]
     sums = [v + pltpu.roll(v, 64, 1) for v in sums]
-    for k in range(0, per, 2):
-        ysend[:, k * 64 : k * 64 + 128] = jnp.where(low, sums[k], sums[k + 1]).astype(BF16)
-    post(peer, nz, 7, lambda w: ysend, yrecv.at[z])
-    yrecv[z] = ysend[...]
+    half = per // 2
+    for h in range(half):
+        ysend[:, h, :] = jnp.where(low, sums[2 * h], sums[2 * h + 1])
+    rz = 32 // nz
+
+    def slab(ref, w):
+        return ref.at[pl.ds(w * rz, rz)]
+
+    post(peer, nz, 7, lambda w: slab(ysend, w), yrecv.at[z])
+    yrecv[z] = ysend[pl.ds(z * rz, rz)]
     land(yrecv, nz, 7)
-    total = yrecv[0].astype(F32)
-    for w in range(1, nz):
-        total = total + yrecv[w].astype(F32)
+    yall[pl.ds(z * rz, rz)] = jnp.sum(yrecv[...], axis=0)
+    post(peer, nz, 11, lambda w: slab(yall, z), slab(yall, z))
+    part = yall.at[pl.ds(0, rz * (nz - 1))]
+    pltpu.make_async_copy(part, part, recv.at[11]).wait()
+    total = jnp.concatenate([yall[:, h, :] for h in range(half)], axis=1)
 
     gw = nt(total, jnp.concatenate([total] * 4, axis=0), HI)
     lane8 = lax.shift_right_logical(iota((8, 128), 1), 5)
@@ -241,17 +260,29 @@
         pair = total[:, (k // 2) * 128 : (k // 2) * 128 + 128]
         other = pltpu.roll(pair, 64, 1)
         blocks.append(jnp.where(low, pair, other) if k % 2 == 0 else jnp.where(low, other, pair))
-    for w in range(pln):
-        val = jnp.zeros((32, 128), F32)
-        for k in range(per):
-            mine = ((x * per + k) * YC + yc).astype(F32)
-            val = val + jnp.where(where_to[w] == mine, blocks[k], 0.0)
-        ssend[w] = val.astype(BF16)
-    post(mate, pln, 9, lambda w: ssend.at[w], srecv.at[m])
-    srecv[m] = ssend[m]
+    blocks = [v.reshape(4, 8, 128) for v in blocks]
+
+    def answer(w):
+        to = goes[w]
+        val = jnp.zeros((4, 8, 128), F32)
+        for v, p in zip(blocks, mine):
+            val = val + jnp.where((to == p)[None], v, 0.0)
+        return val.reshape(32, 128).astype(BF16)
+
+    def reply(k, carry):
+        w, device = mate(k)
+        ssend[w] = answer(w)
+        pltpu.make_async_remote_copy(
+            src_ref=ssend.at[w], dst_ref=srecv.at[m], send_sem=send.at[9], recv_sem=recv.at[9],
+            device_id=device, device_id_type=MESH,
+        ).start()
+        return carry
+
+    lax.fori_loop(1, pln, reply, 0)
+    srecv[m] = answer(m)
     own = jnp.zeros((32, 128), F32)
     for k in range(per):
-        own = own + jnp.where(lax.rem(z, per) == k, blocks[k], 0.0)
+        own = own + jnp.where(lax.rem(z, per) == k, blocks[k].reshape(32, 128), 0.0)
     xsend[...] = own
     post(xmate, nx, 10, lambda w: xsend, xrecv.at[x])
     xrecv[x] = own
@@ -283,8 +314,8 @@
     got = srecv[0].astype(F32)
     for w in range(1, pln):
         got = got + srecv[w].astype(F32)
-    mine = xrecv[lax.div(z, per)]
-    factor_ref[...] = jnp.dot(move, mine[:, 0:64], precision=HI, preferred_element_type=F32)
+    held = xrecv[lax.div(z, per)]
+    factor_ref[...] = jnp.dot(move, held[:, 0:64], precision=HI, preferred_element_type=F32)
     order = jnp.concatenate(
         [mref[pl.ds(0, 16, stride=2), :][:, 0:32], mref[pl.ds(1, 16, stride=2), :][:, 0:32]], axis=0
     )
@@ -303,6 +334,7 @@
     sent(precv, pln, 5)
     sent(zrecv, pln, 6)
     sent(yrecv, nz, 7)
+    pltpu.make_async_copy(part, part, send.at[11]).wait()
     sent(grecv, pln, 8)
     sent(srecv, pln, 9)
     sent(xrecv, nx, 10)
@@ -318,22 +350,28 @@
     def per_device(tiles, block_one, block_two, block_three, owner_map, u_one, u_two, u_three):
         rows_total = owner_map.shape[0] * tiles.shape[1]
         vm = pl.BlockSpec(memory_space=pltpu.VMEM)
-        sm = pl.BlockSpec(memory_space=pltpu.SMEM)
         factor, tf = pl.pallas_call(
             functools.partial(kernel, nx, nz, rows_total),
             out_shape=(
                 jax.ShapeDtypeStruct((32, 64), F32),
                 jax.ShapeDtypeStruct((2, 16, 128), BF16),
             ),
-            in_specs=[pl.BlockSpec(memory_space=pl.ANY), sm, sm, sm, sm, vm, vm, vm],
+            in_specs=[pl.BlockSpec(memory_space=pltpu.HBM)] * 8,
             out_specs=(vm, vm),
             scratch_shapes=[
+                pltpu.SMEM((2,), jnp.int32),
+                pltpu.SMEM((2,), jnp.int32),
+                pltpu.SMEM((2,), jnp.int32),
+                pltpu.SMEM((owner_map.shape[0],), jnp.int32),
+                pltpu.VMEM(u_one.shape, F32),
+                pltpu.VMEM(u_two.shape, BF16),
+                pltpu.VMEM(u_three.shape, BF16),
                 pltpu.VMEM((128, 4096), BF16),
                 pltpu.VMEM((32, 256), F32),
                 pltpu.VMEM((qr, 256), BF16),
                 pltpu.VMEM((nz, qr, 256), BF16),
-                pltpu.VMEM((pln, 48, 128), BF16),
-                pltpu.VMEM((48, 128), BF16),
+                pltpu.VMEM((pln, 32, 128), BF16),
+                pltpu.VMEM((32, 128), BF16),
                 pltpu.VMEM((pln, 32, 128), BF16),
                 pltpu.VMEM((pln, 32, 128), BF16),
                 pltpu.VMEM((32, 64, 128), F32),
@@ -346,8 +384,10 @@
                 pltpu.VMEM((pln, 8, 128), F32),
                 pltpu.VMEM((32, 128), BF16),
                 pltpu.VMEM((pln, 32, 128), BF16),
-                pltpu.VMEM((32, 64 * per), BF16),
-                pltpu.VMEM((nz, 32, 64 * per), BF16),
+                pltpu.VMEM((pln, 8, 128), F32),
+                pltpu.VMEM((32, per // 2, 128), F32),
+                pltpu.VMEM((nz, 32 // nz, per // 2, 128), F32),
+                pltpu.VMEM((32, per // 2, 128), F32),
                 pltpu.VMEM((8, 128), F32),
                 pltpu.VMEM((pln, 8, 128), F32),
                 pltpu.VMEM((pln, 32, 128), BF16),
@@ -355,12 +395,12 @@
                 pltpu.VMEM((32, 128), F32),
                 pltpu.VMEM((nx, 32, 128), F32),
                 pltpu.VMEM((32, 128), F32),
-                pltpu.SemaphoreType.DMA((2,)),
-                pltpu.SemaphoreType.DMA((11,)),
-                pltpu.SemaphoreType.DMA((11,)),
+                pltpu.SemaphoreType.DMA((9,)),
+                pltpu.SemaphoreType.DMA((12,)),
+                pltpu.SemaphoreType.DMA((12,)),
             ],
             compiler_params=pltpu.CompilerParams(
-                collective_id=0, has_side_effects=True, vmem_limit_bytes=32 << 20
+                collective_id=0, has_side_effects=True, vmem_limit_bytes=60 << 20
             ),
             name="hooi_step",
         )(tiles, block_one, block_two, block_three, owner_map, u_one, u_two, u_three)

time: 93.5 us -> 86.3 us (0.923)
  local copies, waits for them, and re-layouts: 7.3 us -> 1.92 us
  Pallas kernels: 85.2 us -> 83.5 us
    unnamed x18 -> x4, local copies, waits for them, and re-layouts: 7.3 us -> 1.92 us
    pallas_call x1, Pallas kernels: 85.2 us -> 83.5 us  [per_device(): pl.pallas_call(functools.partial(kernel, nx, nz, rows_total), out_shape=(...]
where the time goes in v2:
time: 86.3 us; the launch traced here: 86.1 us
  Pallas kernels  83.5 us (97%)
  local copies, waits for them, and re-layouts  1.92 us (2%)
    pallas_call x1, Pallas kernels, per_device(): pl.pallas_call(functools.partial(kernel, nx, nz, rows_total), out_shape=(...  83.5 us
    unnamed x4, local copies, waits for them, and re-layouts  1.92 us

profile of v2, /device:TPU:1, one launch (start us, length us, event | category | flops | bytes accessed | tf_op | source)
XLA Modules:
  0.0 86.1 jit_solution(18340259595561498509)
XLA Ops:
  0.6 83.5 %hooi_step.1 = (f32[32,64]{1,0:T(8,128)}, bf16[2,16,128]{2,1,0:T(8,128)(2,1)}) custom-call(bf16[2,64,4096]{2,1,0:T(8,128)(2,1)} %tiles_ref.1, s32[2]{0:T(128)} %b1_hbm.1, s32[2]{0:T(128)} %b2_hbm.1, s32[2]{0:T(128)} %b3_hbm.1, s32[128]{0:T(128)} %owner_hbm.1, f32[32,64]{1,0:T(8,128)} %u1_hbm.1, bf16[32,128]{1,0:T(8,128)(2,1)} %u2_hbm.1, bf16[32,1024]{1,0:T(8,128)(2,1)} %u3_hbm.1), custom_call_target="tpu_custom_call" | custom-call | tf_op jit(solution)/shard_map/hooi_step/pallas_call | solution.py:353
  84.2 0.0 copy-start
  84.2 1.3 %copy.12 = bf16[1,2,16,128]{3,1,2,0:T(2,128)(2,1)} copy(bf16[1,2,16,128]{3,2,1,0:T(8,128)(2,1)} %bitcast.5) | data formatting | bytes 16384
  85.5 0.0 copy-done
  85.5 0.6 copy.14
Async XLA Ops:
  84.2 1.3 %copy-start = (f32[32,64]{1,0:T(8,128)S(1)}, f32[32,64]{1,0:T(8,128)}, u32[]{:S(2)}) copy-start(f32[32,64]{1,0:T(8,128)} %get-tuple-element.8) | copy-start | bytes 24580

commit v3 on v2

--- a/solution.py
+++ b/solution.py
@@ -31,7 +31,7 @@
     factor_ref, tf_ref,
     b1_ref, b2_ref, b3_ref, owner_ref, u1_ref, u2_ref, u3_ref,
     tl, us, shq, tq, req, reqs, obuf, gbuf, ft, pt, wsend, wrecv, lsend, lrecv, psend, precv,
-    zsend, zrecv, goes, ysend, yrecv, yall, gsend, grecv, ssend, srecv, xsend, xrecv, mref,
+    zsend, zrecv, gosend, goes, ysend, yrecv, yall, gsend, grecv, ssend, srecv, xsend, xrecv, mref,
     tsem, send, recv,
 ):
     pln = nx * YC
@@ -50,47 +50,42 @@
     inputs = [
         pltpu.make_async_copy(src, dst, tsem.at[2 + n])
         for n, (src, dst) in enumerate(
-            ((b1_hbm, b1_ref), (owner_hbm, owner_ref), (b2_hbm, b2_ref), (u2_hbm, u2_ref),
-             (u1_hbm, u1_ref), (b3_hbm, b3_ref), (u3_hbm, u3_ref))
+            ((u2_hbm, u2_ref), (u1_hbm, u1_ref), (b1_hbm, b1_ref), (owner_hbm, owner_ref),
+             (b2_hbm, b2_ref), (b3_hbm, b3_ref), (u3_hbm, u3_ref))
         )
     ]
     for c in inputs + copies:
         c.start()
 
-    def mate(k):
-        w = lax.rem(m + k, pln)
-        return w, {"tiles": z * YC + lax.rem(w, YC), "rep": lax.div(w, YC)}
-
-    def peer(k):
-        w = lax.rem(z + k, nz)
-        return w, {"tiles": w * YC + yc, "rep": x}
-
-    def xmate(k):
-        w = lax.rem(x + k, nx)
-        return w, {"tiles": t_id, "rep": w}
+    def far(d, n):
+        return min(d, n - d)
+
+    xs = [lax.rem(x + d, nx) for d in range(nx)]
+    ys = [lax.rem(lax.div(yc, 2) + d, YC // 2) * 2 for d in range(YC // 2)]
+    cs = [lax.rem(yc, 2), 1 - lax.rem(yc, 2)]
+    steps = [
+        (far(dx, nx) + far(dy, YC // 2), dx, dy, dc)
+        for dx in range(nx) for dy in range(YC // 2) for dc in range(2)
+    ]
+    steps = sorted(steps, reverse=True)[:-1]
+    mates = [
+        (xs[dx] * YC + ys[dy] + cs[dc], {"tiles": z * YC + ys[dy] + cs[dc], "rep": xs[dx]})
+        for _, dx, dy, dc in steps
+    ]
+    zs = [lax.rem(z + d, nz) for d in sorted(range(1, nz), key=lambda d: -far(d, nz))]
+    peers = [(w, {"tiles": w * YC + yc, "rep": x}) for w in zs]
+    xmates = [(w, {"tiles": t_id, "rep": w}) for w in xs[1:]]
 
     barrier = pltpu.get_barrier_semaphore()
-
-    def greet(who, n):
-        def body(k, carry):
-            pl.semaphore_signal(barrier, inc=1, device_id=who(k)[1], device_id_type=MESH)
-            return carry
-
-        lax.fori_loop(1, n, body, 0)
-
-    greet(mate, pln)
-    greet(peer, nz)
-
-    def post(who, n, phase, src, dst):
-        def body(k, carry):
-            w, device = who(k)
+    for _, device in peers + mates:
+        pl.semaphore_signal(barrier, inc=1, device_id=device, device_id_type=MESH)
+
+    def post(who, phase, src, dst):
+        for w, device in who:
             pltpu.make_async_remote_copy(
                 src_ref=src(w), dst_ref=dst, send_sem=send.at[phase], recv_sem=recv.at[phase],
                 device_id=device, device_id_type=MESH,
             ).start()
-            return carry
-
-        lax.fori_loop(1, n, body, 0)
 
     def land(buf, n, phase):
         part = buf.at[pl.ds(0, n - 1)]
@@ -100,7 +95,16 @@
         part = buf.at[pl.ds(0, n - 1)]
         pltpu.make_async_copy(part, part, send.at[phase]).wait()
 
-    for c in inputs:
+    for c in inputs[:2]:
+        c.wait()
+    us[:, pl.ds(0, 128)] = u2_ref[...].astype(F32)
+    us[:, pl.ds(128, 64)] = jnp.zeros((32, 64), F32)
+    us[:, pl.ds(192, 64)] = u1_ref[...]
+    shq[...] = us[pl.ds(pl.multiple_of(x * qr, qr), qr), :].astype(BF16)
+    pl.semaphore_wait(barrier, pln + nz - 2)
+    post(peers, 0, lambda w: shq, tq.at[z])
+
+    for c in inputs[2:]:
         c.wait()
     b2 = [b2_ref[t] for t in range(2)]
     b3 = [b3_ref[t] for t in range(2)]
@@ -111,20 +115,20 @@
 
     def ask(q0, q1):
         want = jnp.where(r16 < qr, q0 * qr, q1 * qr - qr) + r16
-        return jnp.where(l16 == want, 1.0, 0.0).astype(BF16)
-
-    reqs[pl.ds(0, 16), :] = ask(lax.shift_right_logical(b2[0], 4), lax.shift_right_logical(b2[1], 4))
-    reqs[pl.ds(16, 16), :] = ask(lax.shift_right_logical(pos[0], 3), lax.shift_right_logical(pos[1], 3))
-    us[:, pl.ds(0, 128)] = u2_ref[...].astype(F32)
-    us[:, pl.ds(128, 64)] = u1_ref[...]
-    us[:, pl.ds(192, 64)] = jnp.zeros((32, 64), F32)
-    shq[...] = us[pl.ds(pl.multiple_of(x * qr, qr), qr), :].astype(BF16)
-
-    pl.semaphore_wait(barrier, pln + nz - 2)
-    post(peer, nz, 0, lambda w: shq, tq.at[z])
-    post(mate, pln, 1, lambda w: reqs, req.at[m])
+        return jnp.where(l16 == want, 1.0, 0.0)
+
+    ask_two = ask(lax.shift_right_logical(b2[0], 4), lax.shift_right_logical(b2[1], 4))
+    odd = jnp.where(r16 < qr, lax.rem(b2[0], 2), lax.rem(b2[1], 2)) == 1
+    reqs[:, 0:128] = jnp.where(odd, 0.0, ask_two).astype(BF16)
+    reqs[:, 128:256] = jnp.where(odd, ask_two, 0.0).astype(BF16)
+    reqs[:, 256:384] = ask(
+        lax.shift_right_logical(pos[0], 3), lax.shift_right_logical(pos[1], 3)
+    ).astype(BF16)
+    post(mates, 1, lambda w: reqs, req.at[m])
     tq[z] = shq[...]
     req[m] = reqs[...]
+    gosend[...] = jnp.where(iota((8, 128), 1) < 64, pos[0], pos[1]).astype(F32)
+    goes[m] = gosend[...]
 
     lane128 = iota((32, 128), 1)
     spread = jnp.where(iota((256, 32), 0) // 8 == iota((256, 32), 1), 1.0, 0.0).astype(BF16)
@@ -155,48 +159,38 @@
 
     land(tq, nz, 0)
     land(req, pln, 1)
-    table = tq[...].astype(F32).reshape(nz * qr, 256).astype(BF16)
+    table = tq[...].astype(F32).reshape(nz * qr, 256)
+    halves = jnp.concatenate([table[:, 0:128], pltpu.roll(table[:, 0:128], 64, 1)], axis=0)
     two_part = jnp.dot(
-        req[:, 0:16, :].reshape(pln * 16, 128), table[:, 0:128], preferred_element_type=F32
+        req[:, :, 0:256].reshape(pln * 16, 256), halves.astype(BF16), preferred_element_type=F32
     )
     one_part = jnp.dot(
-        req[:, 16:32, :].reshape(pln * 16, 128), table[:, 128:256], preferred_element_type=F32
-    )
-    obuf[:, 0:16, :] = two_part.reshape(pln, 16, 128).astype(BF16)
-    at = jnp.where(r16 < 8, pos[0], pos[1]).astype(F32)
-    one_part = jnp.where(l16 < 64, one_part.reshape(pln, 16, 128), at)
-    obuf[:, 16:32, :] = one_part.astype(BF16)
-    post(mate, pln, 2, lambda w: obuf.at[w], gbuf.at[m])
+        req[:, :, 256:384].reshape(pln * 16, 128), table[:, 128:256].astype(BF16),
+        preferred_element_type=F32,
+    )
+    both = jnp.where(iota((pln * 16, 128), 1) < 64, two_part, one_part)
+    obuf[...] = both.reshape(pln, 16, 128).astype(BF16)
+    post(mates, 2, lambda w: obuf.at[w], gbuf.at[m])
     gbuf[m] = obuf[m]
     land(gbuf, pln, 2)
 
-    r32 = iota((32, 128), 0)
+    held_two = [lax.rem(lax.shift_right_logical(b, 1), YC) for b in b2]
+    held_one = [lax.rem(p, YC) for p in pos]
     holder = jnp.where(
-        r32 < 16,
-        jnp.where(r32 < 8, lax.rem(lax.shift_right_logical(b2[0], 1), YC),
-                  lax.rem(lax.shift_right_logical(b2[1], 1), YC)),
-        jnp.where(r32 < 24, lax.rem(pos[0], YC), lax.rem(pos[1], YC)),
-    )
-    low8 = iota((8, 128), 1) < 64
+        l16 < 64,
+        jnp.where(r16 < 8, held_two[0], held_two[1]),
+        jnp.where(r16 < 8, held_one[0], held_one[1]),
+    )
     parts = []
     for xx in range(nx):
-        acc = jnp.zeros((32, 128), F32)
+        acc = jnp.zeros((16, 128), F32)
         for cc in range(YC):
-            val = gbuf[xx * YC + cc].astype(F32)
-            goes[xx * YC + cc] = jnp.where(low8, pltpu.roll(val[16:24], 64, 1), val[24:32])
-            acc = acc + jnp.where(holder == cc, val, 0.0)
+            acc = acc + jnp.where(holder == cc, gbuf[xx * YC + cc].astype(F32), 0.0)
         parts.append(acc)
-
-    def rows_of(slot):
-        return jnp.concatenate([p[slot * 8 : slot * 8 + 8] for p in parts], axis=0)
-
     low = lane128 < 64
-    two = []
-    for t in range(2):
-        v = rows_of(t)
-        two.append(jnp.where(lax.rem(b2[t], 2) == 1, pltpu.roll(v, 64, 1), v))
-    u2 = jnp.concatenate(two, axis=0)[:, 0:64].astype(BF16)
-    readers = jnp.where(low, rows_of(2), pltpu.roll(rows_of(3), 64, 1)).astype(BF16)
+    picked = [jnp.concatenate([p[t * 8 : t * 8 + 8] for p in parts], axis=0) for t in range(2)]
+    u2 = jnp.concatenate(picked, axis=0)[:, 0:64].astype(BF16)
+    readers = jnp.where(low, pltpu.roll(picked[0], 64, 1), picked[1]).astype(BF16)
 
     for s in range(32):
         d = jnp.dot(u2, ft[s].astype(BF16), preferred_element_type=F32)
@@ -205,24 +199,26 @@
     w_part = nt(readers, pt[...])
     for q in range(8):
         wsend[:, q, :] = w_part[:, q * 128 : (q + 1) * 128]
-    post(mate, pln, 3, lambda w: wsend.at[w], wrecv.at[m])
+    post(mates, 3, lambda w: wsend.at[w], wrecv.at[m])
     wrecv[m] = wsend[m]
     land(wrecv, pln, 3)
     lsend[...] = jnp.sum(wrecv[...], axis=0)
-    post(peer, nz, 4, lambda w: lsend, lrecv.at[z])
+    post(peers, 4, lambda w: lsend, lrecv.at[z])
     lrecv[z] = lsend[...]
+    post(mates, 12, lambda w: gosend, goes.at[m])
     land(lrecv, nz, 4)
     psend[...] = jnp.sum(lrecv[...], axis=0).astype(BF16).astype(F32)
-    post(mate, pln, 5, lambda w: psend, precv.at[m])
+    post(mates, 5, lambda w: psend, precv.at[m])
     precv[m] = psend[...]
     land(precv, pln, 5)
     project = jnp.concatenate([precv[:, q, :].astype(BF16) for q in range(8)], axis=1)
 
     zsend[...] = jnp.dot(project, pt[...], preferred_element_type=F32).astype(BF16)
-    post(mate, pln, 6, lambda w: zsend, zrecv.at[m])
+    post(mates, 6, lambda w: zsend, zrecv.at[m])
     zrecv[m] = zsend[...]
     land(zrecv, pln, 6)
     mine = [((x * per + k) * YC + yc).astype(F32) for k in range(per)]
+    land(goes, pln, 12)
     sums = [jnp.zeros((4, 8, 128), F32) for _ in range(per)]
     for w in range(pln):
         to = goes[w]
@@ -238,11 +234,11 @@
     def slab(ref, w):
         return ref.at[pl.ds(w * rz, rz)]
 
-    post(peer, nz, 7, lambda w: slab(ysend, w), yrecv.at[z])
+    post(peers, 7, lambda w: slab(ysend, w), yrecv.at[z])
     yrecv[z] = ysend[pl.ds(z * rz, rz)]
     land(yrecv, nz, 7)
     yall[pl.ds(z * rz, rz)] = jnp.sum(yrecv[...], axis=0)
-    post(peer, nz, 11, lambda w: slab(yall, z), slab(yall, z))
+    post(peers, 11, lambda w: slab(yall, z), slab(yall, z))
     part = yall.at[pl.ds(0, rz * (nz - 1))]
     pltpu.make_async_copy(part, part, recv.at[11]).wait()
     total = jnp.concatenate([yall[:, h, :] for h in range(half)], axis=1)
@@ -253,7 +249,7 @@
     for q in range(4):
         packed = packed + jnp.where(lane8 == q, gw[q * 8 : q * 8 + 8], 0.0)
     gsend[...] = packed
-    post(mate, pln, 8, lambda w: gsend, grecv.at[m])
+    post(mates, 8, lambda w: gsend, grecv.at[m])
     grecv[m] = packed
     blocks = []
     for k in range(per):
@@ -269,23 +265,19 @@
             val = val + jnp.where((to == p)[None], v, 0.0)
         return val.reshape(32, 128).astype(BF16)
 
-    def reply(k, carry):
-        w, device = mate(k)
+    for w, device in mates:
         ssend[w] = answer(w)
         pltpu.make_async_remote_copy(
             src_ref=ssend.at[w], dst_ref=srecv.at[m], send_sem=send.at[9], recv_sem=recv.at[9],
             device_id=device, device_id_type=MESH,
         ).start()
-        return carry
-
-    lax.fori_loop(1, pln, reply, 0)
     srecv[m] = answer(m)
     own = jnp.zeros((32, 128), F32)
     for k in range(per):
         own = own + jnp.where(lax.rem(z, per) == k, blocks[k].reshape(32, 128), 0.0)
-    xsend[...] = own
-    post(xmate, nx, 10, lambda w: xsend, xrecv.at[x])
-    xrecv[x] = own
+    xsend[...] = jnp.where(low[0:16], own[0:16], own[16:32])
+    post(xmates, 10, lambda w: xsend, xrecv.at[x])
+    xrecv[x] = xsend[...]
 
     land(grecv, pln, 8)
     packed = jnp.sum(grecv[...], axis=0)
@@ -315,6 +307,7 @@
     for w in range(1, pln):
         got = got + srecv[w].astype(F32)
     held = xrecv[lax.div(z, per)]
+    held = jnp.concatenate([held, pltpu.roll(held, 64, 1)], axis=0)
     factor_ref[...] = jnp.dot(move, held[:, 0:64], precision=HI, preferred_element_type=F32)
     order = jnp.concatenate(
         [mref[pl.ds(0, 16, stride=2), :][:, 0:32], mref[pl.ds(1, 16, stride=2), :][:, 0:32]], axis=0
@@ -338,6 +331,7 @@
     sent(grecv, pln, 8)
     sent(srecv, pln, 9)
     sent(xrecv, nx, 10)
+    sent(goes, pln, 12)
 
 
 def solution(mesh):
@@ -370,10 +364,10 @@
                 pltpu.VMEM((32, 256), F32),
                 pltpu.VMEM((qr, 256), BF16),
                 pltpu.VMEM((nz, qr, 256), BF16),
-                pltpu.VMEM((pln, 32, 128), BF16),
-                pltpu.VMEM((32, 128), BF16),
-                pltpu.VMEM((pln, 32, 128), BF16),
-                pltpu.VMEM((pln, 32, 128), BF16),
+                pltpu.VMEM((pln, 16, 384), BF16),
+                pltpu.VMEM((16, 384), BF16),
+                pltpu.VMEM((pln, 16, 128), BF16),
+                pltpu.VMEM((pln, 16, 128), BF16),
                 pltpu.VMEM((32, 64, 128), F32),
                 pltpu.VMEM((1024, 128), BF16),
                 pltpu.VMEM((pln, 8, 128), F32),
@@ -384,6 +378,7 @@
                 pltpu.VMEM((pln, 8, 128), F32),
                 pltpu.VMEM((32, 128), BF16),
                 pltpu.VMEM((pln, 32, 128), BF16),
+                pltpu.VMEM((8, 128), F32),
                 pltpu.VMEM((pln, 8, 128), F32),
                 pltpu.VMEM((32, per // 2, 128), F32),
                 pltpu.VMEM((nz, 32 // nz, per // 2, 128), F32),
@@ -392,12 +387,12 @@
                 pltpu.VMEM((pln, 8, 128), F32),
                 pltpu.VMEM((pln, 32, 128), BF16),
                 pltpu.VMEM((pln, 32, 128), BF16),
-                pltpu.VMEM((32, 128), F32),
-                pltpu.VMEM((nx, 32, 128), F32),
+                pltpu.VMEM((16, 128), F32),
+                pltpu.VMEM((nx, 16, 128), F32),
                 pltpu.VMEM((32, 128), F32),
                 pltpu.SemaphoreType.DMA((9,)),
-                pltpu.SemaphoreType.DMA((12,)),
-                pltpu.SemaphoreType.DMA((12,)),
+                pltpu.SemaphoreType.DMA((13,)),
+                pltpu.SemaphoreType.DMA((13,)),
             ],
             compiler_params=pltpu.CompilerParams(
                 collective_id=0, has_side_effects=True, vmem_limit_bytes=60 << 20

time: 86.3 us -> 78.2 us (0.906)
  Pallas kernels: 83.5 us -> 75.4 us
    pallas_call x1, Pallas kernels: 83.5 us -> 75.4 us  [per_device(): pl.pallas_call(functools.partial(kernel, nx, nz, rows_total), out_shape=(...]
where the time goes in v3:
time: 78.2 us; the launch traced here: 78 us
  Pallas kernels  75.4 us (96%)
  local copies, waits for them, and re-layouts  1.92 us (2%)
    pallas_call x1, Pallas kernels, per_device(): pl.pallas_call(functools.partial(kernel, nx, nz, rows_total), out_shape=(...  75.4 us
    unnamed x4, local copies, waits for them, and re-layouts  1.92 us

profile of v3, /device:TPU:1, one launch (start us, length us, event | category | flops | bytes accessed | tf_op | source)
XLA Modules:
  0.0 78.0 jit_solution(9771320101918661241)
XLA Ops:
  0.6 75.4 %hooi_step.1 = (f32[32,64]{1,0:T(8,128)}, bf16[2,16,128]{2,1,0:T(8,128)(2,1)}) custom-call(bf16[2,64,4096]{2,1,0:T(8,128)(2,1)} %tiles_ref.1, s32[2]{0:T(128)} %b1_hbm.1, s32[2]{0:T(128)} %b2_hbm.1, s32[2]{0:T(128)} %b3_hbm.1, s32[128]{0:T(128)} %owner_hbm.1, f32[32,64]{1,0:T(8,128)} %u1_hbm.1, bf16[32,128]{1,0:T(8,128)(2,1)} %u2_hbm.1, bf16[32,1024]{1,0:T(8,128)(2,1)} %u3_hbm.1), custom_call_target="tpu_custom_call" | custom-call | tf_op jit(solution)/shard_map/hooi_step/pallas_call | solution.py:347
  76.1 0.0 copy-start
  76.1 1.3 %copy.12 = bf16[1,2,16,128]{3,1,2,0:T(2,128)(2,1)} copy(bf16[1,2,16,128]{3,2,1,0:T(8,128)(2,1)} %bitcast.5) | data formatting | bytes 16384
  77.4 0.0 copy-done
  77.4 0.6 copy.14
Async XLA Ops:
  76.1 1.3 %copy-start = (f32[32,64]{1,0:T(8,128)S(1)}, f32[32,64]{1,0:T(8,128)}, u32[]{:S(2)}) copy-start(f32[32,64]{1,0:T(8,128)} %get-tuple-element.8) | copy-start | bytes 24580

commit v4 on v3

--- a/solution.py
+++ b/solution.py
@@ -8,7 +8,6 @@
 from jax.sharding import PartitionSpec as P
 
 MESH = pl.DeviceIdType.MESH
-NS_STEPS = 2
 YC = 8
 F32 = jnp.float32
 BF16 = jnp.bfloat16
@@ -54,8 +53,6 @@
              (b2_hbm, b2_ref), (b3_hbm, b3_ref), (u3_hbm, u3_ref))
         )
     ]
-    for c in inputs + copies:
-        c.start()
 
     def far(d, n):
         return min(d, n - d)
@@ -79,6 +76,8 @@
     barrier = pltpu.get_barrier_semaphore()
     for _, device in peers + mates:
         pl.semaphore_signal(barrier, inc=1, device_id=device, device_id_type=MESH)
+    for c in inputs + copies:
+        c.start()
 
     def post(who, phase, src, dst):
         for w, device in who:
@@ -243,7 +242,8 @@
     pltpu.make_async_copy(part, part, recv.at[11]).wait()
     total = jnp.concatenate([yall[:, h, :] for h in range(half)], axis=1)
 
-    gw = nt(total, jnp.concatenate([total] * 4, axis=0), HI)
+    rounded = total.astype(BF16)
+    gw = nt(rounded, jnp.concatenate([rounded] * 4, axis=0))
     lane8 = lax.shift_right_logical(iota((8, 128), 1), 5)
     packed = jnp.zeros((8, 128), F32)
     for q in range(4):
@@ -290,15 +290,11 @@
     trace = jnp.sum(jnp.sum(g0 * eye, axis=1, keepdims=True), axis=0, keepdims=True)
     inv = 1.0 / jnp.sqrt(trace / rows_total + 1e-06)
     g = g0 * (inv * inv) / rows_total
-    move = eye * inv
-    for step in range(NS_STEPS):
-        if step > 0:
-            g = jnp.dot(
-                jnp.dot(a, g, precision=HI, preferred_element_type=F32), a,
-                precision=HI, preferred_element_type=F32,
-            )
-        a = 1.5 * eye - 0.5 * g
-        move = jnp.dot(a, move, precision=HI, preferred_element_type=F32)
+    a0 = 1.5 * eye - 0.5 * g
+    g2 = jnp.dot(g, g, precision=HI, preferred_element_type=F32)
+    a0a0 = 2.25 * eye - 1.5 * g + 0.25 * g2
+    a0g = 1.5 * g - 0.5 * g2
+    move = inv * (1.5 * a0 - 0.5 * jnp.dot(a0a0, a0g, precision=HI, preferred_element_type=F32))
     mref[:, 0:32] = move
 
     land(srecv, pln, 9)
@@ -347,8 +343,8 @@
         factor, tf = pl.pallas_call(
             functools.partial(kernel, nx, nz, rows_total),
             out_shape=(
-                jax.ShapeDtypeStruct((32, 64), F32),
-                jax.ShapeDtypeStruct((2, 16, 128), BF16),
+                pltpu.VMEM((32, 64), F32),
+                pltpu.VMEM((2, 16, 128), BF16),
             ),
             in_specs=[pl.BlockSpec(memory_space=pltpu.HBM)] * 8,
             out_specs=(vm, vm),

time: 78.2 us -> 76.6 us (0.980)
  Pallas kernels: 75.4 us -> 74.6 us
    pallas_call x1, Pallas kernels: 75.4 us -> 74.6 us  [per_device(): pl.pallas_call(functools.partial(kernel, nx, nz, rows_total), out_shape=(...]
    unnamed x4 -> x2, local copies, waits for them, and re-layouts: 1.92 us -> 1.21 us
where the time goes in v4:
time: 76.6 us; the launch traced here: 76.5 us
  Pallas kernels  74.6 us (97%)
  local copies, waits for them, and re-layouts  1.21 us (2%)
    pallas_call x1, Pallas kernels, per_device(): pl.pallas_call(functools.partial(kernel, nx, nz, rows_total), out_shape=(...  74.6 us

profile of v4, /device:TPU:1, one launch (start us, length us, event | category | flops | bytes accessed | tf_op | source)
XLA Modules:
  0.0 76.5 jit_solution(2676950903742979633)
XLA Ops:
  0.6 74.6 %hooi_step.1 = (f32[32,64]{1,0:T(8,128)S(1)}, bf16[2,16,128]{2,1,0:T(8,128)(2,1)S(1)}) custom-call(bf16[2,64,4096]{2,1,0:T(8,128)(2,1)} %tiles_ref.1, s32[2]{0:T(128)} %b1_hbm.1, s32[2]{0:T(128)} %b2_hbm.1, s32[2]{0:T(128)} %b3_hbm.1, s32[128]{0:T(128)} %owner_hbm.1, f32[32,64]{1,0:T(8,128)} %u1_hbm.1, bf16[32,128]{1,0:T(8,128)(2,1)} %u2_hbm.1, ...), custom_call_target="tpu_custom_call" | custom-call | tf_op jit(solution)/shard_map/hooi_step/pallas_call | solution.py:343
  75.3 0.6 copy.14
  75.9 0.6 copy.12

commit v5 on v4

--- a/solution.py
+++ b/solution.py
@@ -29,7 +29,7 @@
     tiles_ref, b1_hbm, b2_hbm, b3_hbm, owner_hbm, u1_hbm, u2_hbm, u3_hbm,
     factor_ref, tf_ref,
     b1_ref, b2_ref, b3_ref, owner_ref, u1_ref, u2_ref, u3_ref,
-    tl, us, shq, tq, req, reqs, obuf, gbuf, ft, pt, wsend, wrecv, lsend, lrecv, psend, precv,
+    tl, us, shq, tq, req, reqs, obuf, gbuf, ft, pt, wsend, whalf, wrecv, lsend, lrecv, psend, precv,
     zsend, zrecv, gosend, goes, ysend, yrecv, yall, gsend, grecv, ssend, srecv, xsend, xrecv, mref,
     tsem, send, recv,
 ):
@@ -198,19 +198,21 @@
     w_part = nt(readers, pt[...])
     for q in range(8):
         wsend[:, q, :] = w_part[:, q * 128 : (q + 1) * 128]
-    post(mates, 3, lambda w: wsend.at[w], wrecv.at[m])
-    wrecv[m] = wsend[m]
+    whalf[...] = wsend[...].astype(BF16)
+    post(mates, 3, lambda w: whalf.at[w], wrecv.at[m])
+    wrecv[m] = whalf[m]
     land(wrecv, pln, 3)
-    lsend[...] = jnp.sum(wrecv[...], axis=0)
+    lsend[...] = jnp.sum(wrecv[...].astype(F32), axis=0).astype(BF16)
     post(peers, 4, lambda w: lsend, lrecv.at[z])
     lrecv[z] = lsend[...]
     post(mates, 12, lambda w: gosend, goes.at[m])
     land(lrecv, nz, 4)
-    psend[...] = jnp.sum(lrecv[...], axis=0).astype(BF16).astype(F32)
+    psend[...] = jnp.sum(lrecv[...].astype(F32), axis=0).astype(BF16)
     post(mates, 5, lambda w: psend, precv.at[m])
     precv[m] = psend[...]
     land(precv, pln, 5)
-    project = jnp.concatenate([precv[:, q, :].astype(BF16) for q in range(8)], axis=1)
+    wsend[...] = precv[...].astype(F32)
+    project = jnp.concatenate([wsend[:, q, :].astype(BF16) for q in range(8)], axis=1)
 
     zsend[...] = jnp.dot(project, pt[...], preferred_element_type=F32).astype(BF16)
     post(mates, 6, lambda w: zsend, zrecv.at[m])
@@ -367,11 +369,12 @@
                 pltpu.VMEM((32, 64, 128), F32),
                 pltpu.VMEM((1024, 128), BF16),
                 pltpu.VMEM((pln, 8, 128), F32),
-                pltpu.VMEM((pln, 8, 128), F32),
-                pltpu.VMEM((8, 128), F32),
-                pltpu.VMEM((nz, 8, 128), F32),
-                pltpu.VMEM((8, 128), F32),
-                pltpu.VMEM((pln, 8, 128), F32),
+                pltpu.VMEM((pln, 8, 128), BF16),
+                pltpu.VMEM((pln, 8, 128), BF16),
+                pltpu.VMEM((8, 128), BF16),
+                pltpu.VMEM((nz, 8, 128), BF16),
+                pltpu.VMEM((8, 128), BF16),
+                pltpu.VMEM((pln, 8, 128), BF16),
                 pltpu.VMEM((32, 128), BF16),
                 pltpu.VMEM((pln, 32, 128), BF16),
                 pltpu.VMEM((8, 128), F32),

time: 76.6 us -> 76.1 us (level)
  no operation moved by 1% of the time
where the time goes in v5:
time: 76.1 us; the launch traced here: 75.9 us
  Pallas kernels  74.1 us (97%)
  local copies, waits for them, and re-layouts  1.21 us (2%)
    pallas_call x1, Pallas kernels, per_device(): pl.pallas_call(functools.partial(kernel, nx, nz, rows_total), out_shape=(...  74.1 us

profile of v5, /device:TPU:1, one launch (start us, length us, event | category | flops | bytes accessed | tf_op | source)
XLA Modules:
  0.0 75.9 jit_solution(6788250561592974119)
XLA Ops:
  0.6 74.1 %hooi_step.1 = (f32[32,64]{1,0:T(8,128)S(1)}, bf16[2,16,128]{2,1,0:T(8,128)(2,1)S(1)}) custom-call(bf16[2,64,4096]{2,1,0:T(8,128)(2,1)} %tiles_ref.1, s32[2]{0:T(128)} %b1_hbm.1, s32[2]{0:T(128)} %b2_hbm.1, s32[2]{0:T(128)} %b3_hbm.1, s32[128]{0:T(128)} %owner_hbm.1, f32[32,64]{1,0:T(8,128)} %u1_hbm.1, bf16[32,128]{1,0:T(8,128)(2,1)} %u2_hbm.1, ...), custom_call_target="tpu_custom_call" | custom-call | tf_op jit(solution)/shard_map/hooi_step/pallas_call | solution.py:345
  74.7 0.6 copy.14
  75.3 0.6 copy.12

commit v6 on v5

--- a/solution.py
+++ b/solution.py
@@ -73,8 +73,15 @@
     peers = [(w, {"tiles": w * YC + yc, "rep": x}) for w in zs]
     xmates = [(w, {"tiles": t_id, "rep": w}) for w in xs[1:]]
 
+    near = nz // 4
+
+    def along(d):
+        return {"tiles": lax.rem(z + d + nz, nz) * YC + yc, "rep": x}
+
+    close = [((nz - d) % nz, along(d)) for k in range(near, 0, -1) for d in (k, -k)]
+
     barrier = pltpu.get_barrier_semaphore()
-    for _, device in peers + mates:
+    for _, device in close + mates:
         pl.semaphore_signal(barrier, inc=1, device_id=device, device_id_type=MESH)
     for c in inputs + copies:
         c.start()
@@ -100,8 +107,12 @@
     us[:, pl.ds(128, 64)] = jnp.zeros((32, 64), F32)
     us[:, pl.ds(192, 64)] = u1_ref[...]
     shq[...] = us[pl.ds(pl.multiple_of(x * qr, qr), qr), :].astype(BF16)
-    pl.semaphore_wait(barrier, pln + nz - 2)
-    post(peers, 0, lambda w: shq, tq.at[z])
+    pl.semaphore_wait(barrier, pln - 1 + 2 * near)
+    for slot, device in close:
+        pltpu.make_async_remote_copy(
+            src_ref=shq, dst_ref=tq.at[slot], send_sem=send.at[0], recv_sem=recv.at[0],
+            device_id=device, device_id_type=MESH,
+        ).start()
 
     for c in inputs[2:]:
         c.wait()
@@ -116,15 +127,20 @@
         want = jnp.where(r16 < qr, q0 * qr, q1 * qr - qr) + r16
         return jnp.where(l16 == want, 1.0, 0.0)
 
-    ask_two = ask(lax.shift_right_logical(b2[0], 4), lax.shift_right_logical(b2[1], 4))
+    def slot_of(at):
+        return lax.rem(at - z + nz, nz)
+
+    ask_two = ask(
+        slot_of(lax.shift_right_logical(b2[0], 4)), slot_of(lax.shift_right_logical(b2[1], 4))
+    )
     odd = jnp.where(r16 < qr, lax.rem(b2[0], 2), lax.rem(b2[1], 2)) == 1
     reqs[:, 0:128] = jnp.where(odd, 0.0, ask_two).astype(BF16)
     reqs[:, 128:256] = jnp.where(odd, ask_two, 0.0).astype(BF16)
     reqs[:, 256:384] = ask(
-        lax.shift_right_logical(pos[0], 3), lax.shift_right_logical(pos[1], 3)
+        slot_of(lax.shift_right_logical(pos[0], 3)), slot_of(lax.shift_right_logical(pos[1], 3))
     ).astype(BF16)
     post(mates, 1, lambda w: reqs, req.at[m])
-    tq[z] = shq[...]
+    tq[0] = shq[...]
     req[m] = reqs[...]
     gosend[...] = jnp.where(iota((8, 128), 1) < 64, pos[0], pos[1]).astype(F32)
     goes[m] = gosend[...]
@@ -156,8 +172,15 @@
         out = jnp.where(low256, nt(diag[0], block), nt(diag[1], block))
         ft[:, jc * 8 : (jc + 1) * 8, :] = out.reshape(32, 8, 128)
 
-    land(tq, nz, 0)
+    land(tq, 2 * near + 1, 0)
+    for src, dst, count, d in ((1, near + 1, near, -near), (nz - near + 1, 2 * near + 1, near - 1, near)):
+        pltpu.make_async_remote_copy(
+            src_ref=tq.at[pl.ds(src, count)], dst_ref=tq.at[pl.ds(dst, count)],
+            send_sem=send.at[13], recv_sem=recv.at[13],
+            device_id=along(d), device_id_type=MESH,
+        ).start()
     land(req, pln, 1)
+    land(tq, 2 * near, 13)
     table = tq[...].astype(F32).reshape(nz * qr, 256)
     halves = jnp.concatenate([table[:, 0:128], pltpu.roll(table[:, 0:128], 64, 1)], axis=0)
     two_part = jnp.dot(
@@ -317,7 +340,8 @@
         v = jnp.dot(order, both, precision=HI, preferred_element_type=F32)
         tf_ref[t] = jnp.where(low16, v[0:16], v[16:32]).astype(BF16)
 
-    sent(tq, nz, 0)
+    sent(tq, 2 * near + 1, 0)
+    sent(tq, 2 * near, 13)
     sent(req, pln, 1)
     sent(gbuf, pln, 2)
     sent(wrecv, pln, 3)
@@ -390,8 +414,8 @@
                 pltpu.VMEM((nx, 16, 128), F32),
                 pltpu.VMEM((32, 128), F32),
                 pltpu.SemaphoreType.DMA((9,)),
-                pltpu.SemaphoreType.DMA((13,)),
-                pltpu.SemaphoreType.DMA((13,)),
+                pltpu.SemaphoreType.DMA((14,)),
+                pltpu.SemaphoreType.DMA((14,)),
             ],
             compiler_params=pltpu.CompilerParams(
                 collective_id=0, has_side_effects=True, vmem_limit_bytes=60 << 20

time: 76.1 us -> 75.5 us (level)
  no operation moved by 1% of the time
where the time goes in v6:
time: 75.5 us; the launch traced here: 75.4 us
  Pallas kernels  73.5 us (97%)
  local copies, waits for them, and re-layouts  1.21 us (2%)
    pallas_call x1, Pallas kernels, per_device(): pl.pallas_call(functools.partial(kernel, nx, nz, rows_total), out_shape=(...  73.5 us

profile of v6, /device:TPU:1, one launch (start us, length us, event | category | flops | bytes accessed | tf_op | source)
XLA Modules:
  0.0 75.4 jit_solution(9307181441721022983)
XLA Ops:
  0.6 73.5 %hooi_step.1 = (f32[32,64]{1,0:T(8,128)S(1)}, bf16[2,16,128]{2,1,0:T(8,128)(2,1)S(1)}) custom-call(bf16[2,64,4096]{2,1,0:T(8,128)(2,1)} %tiles_ref.1, s32[2]{0:T(128)} %b1_hbm.1, s32[2]{0:T(128)} %b2_hbm.1, s32[2]{0:T(128)} %b3_hbm.1, s32[128]{0:T(128)} %owner_hbm.1, f32[32,64]{1,0:T(8,128)} %u1_hbm.1, bf16[32,128]{1,0:T(8,128)(2,1)} %u2_hbm.1, ...), custom_call_target="tpu_custom_call" | custom-call | tf_op jit(solution)/shard_map/hooi_step/pallas_call | solution.py:369
  74.2 0.6 copy.14
  74.8 0.6 copy.12

commit v7 on v6

--- a/solution.py
+++ b/solution.py
@@ -81,9 +81,11 @@
     close = [((nz - d) % nz, along(d)) for k in range(near, 0, -1) for d in (k, -k)]
 
     barrier = pltpu.get_barrier_semaphore()
+    for c in inputs[:2]:
+        c.start()
     for _, device in close + mates:
         pl.semaphore_signal(barrier, inc=1, device_id=device, device_id_type=MESH)
-    for c in inputs + copies:
+    for c in inputs[2:] + copies:
         c.start()
 
     def post(who, phase, src, dst):
@@ -168,17 +170,18 @@
         c.wait()
     low256 = iota((256, 128), 1) < 64
     for jc in range(8):
+        if jc == 4:
+            land(tq, 2 * near + 1, 0)
+            for src, dst, count, d in ((1, near + 1, near, -near), (nz - near + 1, 2 * near + 1, near - 1, near)):
+                pltpu.make_async_remote_copy(
+                    src_ref=tq.at[pl.ds(src, count)], dst_ref=tq.at[pl.ds(dst, count)],
+                    send_sem=send.at[13], recv_sem=recv.at[13],
+                    device_id=along(d), device_id_type=MESH,
+                ).start()
         block = tl[:, jc * 512 : (jc + 1) * 512]
         out = jnp.where(low256, nt(diag[0], block), nt(diag[1], block))
         ft[:, jc * 8 : (jc + 1) * 8, :] = out.reshape(32, 8, 128)
 
-    land(tq, 2 * near + 1, 0)
-    for src, dst, count, d in ((1, near + 1, near, -near), (nz - near + 1, 2 * near + 1, near - 1, near)):
-        pltpu.make_async_remote_copy(
-            src_ref=tq.at[pl.ds(src, count)], dst_ref=tq.at[pl.ds(dst, count)],
-            send_sem=send.at[13], recv_sem=recv.at[13],
-            device_id=along(d), device_id_type=MESH,
-        ).start()
     land(req, pln, 1)
     land(tq, 2 * near, 13)
     table = tq[...].astype(F32).reshape(nz * qr, 256)

time: 75.5 us -> 75.5 us (level)
  no operation moved by 1% of the time
where the time goes in v7:
time: 75.5 us; the launch traced here: 75.4 us
  Pallas kernels  73.5 us (97%)
  local copies, waits for them, and re-layouts  1.21 us (2%)
    pallas_call x1, Pallas kernels, per_device(): pl.pallas_call(functools.partial(kernel, nx, nz, rows_total), out_shape=(...  73.5 us

profile of v7, /device:TPU:1, one launch (start us, length us, event | category | flops | bytes accessed | tf_op | source)
XLA Modules:
  0.0 75.4 jit_solution(10567605736793100791)
XLA Ops:
  0.6 73.5 %hooi_step.1 = (f32[32,64]{1,0:T(8,128)S(1)}, bf16[2,16,128]{2,1,0:T(8,128)(2,1)S(1)}) custom-call(bf16[2,64,4096]{2,1,0:T(8,128)(2,1)} %tiles_ref.1, s32[2]{0:T(128)} %b1_hbm.1, s32[2]{0:T(128)} %b2_hbm.1, s32[2]{0:T(128)} %b3_hbm.1, s32[128]{0:T(128)} %owner_hbm.1, f32[32,64]{1,0:T(8,128)} %u1_hbm.1, bf16[32,128]{1,0:T(8,128)(2,1)} %u2_hbm.1, ...), custom_call_target="tpu_custom_call" | custom-call | tf_op jit(solution)/shard_map/hooi_step/pallas_call | solution.py:372
  74.2 0.6 copy.14
  74.8 0.6 copy.12

commit v8 on v7

--- a/solution.py
+++ b/solution.py
@@ -146,6 +146,7 @@
     req[m] = reqs[...]
     gosend[...] = jnp.where(iota((8, 128), 1) < 64, pos[0], pos[1]).astype(F32)
     goes[m] = gosend[...]
+    post(mates, 12, lambda w: gosend, goes.at[m])
 
     lane128 = iota((32, 128), 1)
     spread = jnp.where(iota((256, 32), 0) // 8 == iota((256, 32), 1), 1.0, 0.0).astype(BF16)
@@ -231,7 +232,6 @@
     lsend[...] = jnp.sum(wrecv[...].astype(F32), axis=0).astype(BF16)
     post(peers, 4, lambda w: lsend, lrecv.at[z])
     lrecv[z] = lsend[...]
-    post(mates, 12, lambda w: gosend, goes.at[m])
     land(lrecv, nz, 4)
     psend[...] = jnp.sum(lrecv[...].astype(F32), axis=0).astype(BF16)
     post(mates, 5, lambda w: psend, precv.at[m])

time: 75.5 us -> 75.5 us (level)
  no operation moved by 1% of the time
where the time goes in v8:
time: 75.5 us; the launch traced here: 75.4 us
  Pallas kernels  73.5 us (97%)
  local copies, waits for them, and re-layouts  1.21 us (2%)
    pallas_call x1, Pallas kernels, per_device(): pl.pallas_call(functools.partial(kernel, nx, nz, rows_total), out_shape=(...  73.5 us

profile of v8, /device:TPU:1, one launch (start us, length us, event | category | flops | bytes accessed | tf_op | source)
XLA Modules:
  0.0 75.4 jit_solution(1387292435050949265)
XLA Ops:
  0.6 73.5 %hooi_step.1 = (f32[32,64]{1,0:T(8,128)S(1)}, bf16[2,16,128]{2,1,0:T(8,128)(2,1)S(1)}) custom-call(bf16[2,64,4096]{2,1,0:T(8,128)(2,1)} %tiles_ref.1, s32[2]{0:T(128)} %b1_hbm.1, s32[2]{0:T(128)} %b2_hbm.1, s32[2]{0:T(128)} %b3_hbm.1, s32[128]{0:T(128)} %owner_hbm.1, f32[32,64]{1,0:T(8,128)} %u1_hbm.1, bf16[32,128]{1,0:T(8,128)(2,1)} %u2_hbm.1, ...), custom_call_target="tpu_custom_call" | custom-call | tf_op jit(solution)/shard_map/hooi_step/pallas_call | solution.py:372
  74.2 0.6 copy.14
  74.8 0.6 copy.12

commit v9 on v5

--- a/solution.py
+++ b/solution.py
@@ -74,9 +74,11 @@
     xmates = [(w, {"tiles": t_id, "rep": w}) for w in xs[1:]]
 
     barrier = pltpu.get_barrier_semaphore()
+    for c in inputs[:2]:
+        c.start()
     for _, device in peers + mates:
         pl.semaphore_signal(barrier, inc=1, device_id=device, device_id_type=MESH)
-    for c in inputs + copies:
+    for c in inputs[2:] + copies:
         c.start()
 
     def post(who, phase, src, dst):

time: 76.1 us -> 76 us (level)
  no operation moved by 1% of the time
where the time goes in v9:
time: 76 us; the launch traced here: 75.9 us
  Pallas kernels  74 us (97%)
  local copies, waits for them, and re-layouts  1.21 us (2%)
    pallas_call x1, Pallas kernels, per_device(): pl.pallas_call(functools.partial(kernel, nx, nz, rows_total), out_shape=(...  74 us

profile of v9, /device:TPU:1, one launch (start us, length us, event | category | flops | bytes accessed | tf_op | source)
XLA Modules:
  0.0 75.9 jit_solution(13636361125550600819)
XLA Ops:
  0.6 74.0 %hooi_step.1 = (f32[32,64]{1,0:T(8,128)S(1)}, bf16[2,16,128]{2,1,0:T(8,128)(2,1)S(1)}) custom-call(bf16[2,64,4096]{2,1,0:T(8,128)(2,1)} %tiles_ref.1, s32[2]{0:T(128)} %b1_hbm.1, s32[2]{0:T(128)} %b2_hbm.1, s32[2]{0:T(128)} %b3_hbm.1, s32[128]{0:T(128)} %owner_hbm.1, f32[32,64]{1,0:T(8,128)} %u1_hbm.1, bf16[32,128]{1,0:T(8,128)(2,1)} %u2_hbm.1, ...), custom_call_target="tpu_custom_call" | custom-call | tf_op jit(solution)/shard_map/hooi_step/pallas_call | solution.py:347
  74.6 0.6 copy.14
  75.2 0.6 copy.12
